TPU v7x, 128 devices: a whole 4x4x4 slice. The times are simulated.
128 devices in a mesh: cfg: 2 (over y_hi), group: 16 (over y_lo, x, core), mp: 4 (over z).
Axes of the slice: x: 4, y: 4 (y_hi: 2, y_lo: 2; y = y_hi * 2 + y_lo), z: 4, core: 2. Of those that a mesh axis runs over, the one named last changes fastest.
Arguments:
- latents: float32 [16384, 64], P(('group', 'mp')), may hold values from -0.6 to 0.6
- text_hidden: bfloat16 [2, 8192, 3072], P('cfg', ('group', 'mp')), may hold values from -6 to 6
- w_img_in: bfloat16 [64, 3072], replicated, may hold values from -0.75 to 0.75
- w_img_qkv: bfloat16 [3072, 4608], P(None, 'mp'), may hold values from -1 to 1
- w_txt_kv: bfloat16 [3072, 3072], P(None, 'mp'), may hold values from -0.109375 to 0.109375
- q_gain: float32 [128], replicated, may hold values from 0.25 to 1.75
- k_gain: float32 [128], replicated, may hold values from 0.25 to 1.75
- w_out: bfloat16 [1536, 3072], replicated, may hold values from -1 to 1
- w_final: bfloat16 [3072, 64], replicated, may hold values from -0.109375 to 0.109375
- mod_img: float32 [8, 3, 3072], replicated, may hold values from -3 to 3
- mod_txt: float32 [8, 2, 3072], replicated, may hold values from -3 to 3
- mod_final: float32 [8, 2, 3072], replicated, may hold values from -3 to 3
- guide: float32 [16], replicated, may hold values from 1.5 to 5
- step_size: float32 [8], replicated, may hold values from 0.02 to 0.3
- img_len: int32 [16], replicated, may hold values from 1 to 1024, as said below
- txt_len: int32 [16], replicated, may hold values from 1 to 512, as said below
- split_flag: int32 [2, 16], replicated, may hold values from 0 to 1, as said below
- tstep: int32 [16], replicated, may hold values from 0 to 7
Outputs:
- velocity: float32 [2, 8192, 64], P('cfg', ('group', 'mp'))
- next_latents: float32 [2, 8192, 64], P('cfg', ('group', 'mp'))
Inputs may be any that keep to these rules, and one draw needn't show every extreme that they name: `img_len`: some group has exactly 1024 live image tokens. `txt_len`: some group has exactly 512 live text tokens. `split_flag`: entries [c, 2j] and [c, 2j + 1] are equal; at least one such pair carries 1 and at least one carries 0.
All inputs are finite; a program needn't handle non-finite values.
Results may differ from a plain program's by a relative error of at most 0.035.
Values may be sent and summed in bfloat16 or wider, within the bound.
A program may use at most 192 MiB of HBM per device.

v0:
```python
import jax
import jax.numpy as jnp
from jax import lax
from jax.sharding import PartitionSpec as P

HD = 128


def partner(value, axis, bit):
    mask = 2**bit
    pairs = [(source, source ^ mask) for source in range(lax.axis_size(axis))]
    return lax.ppermute(value, axis, pairs)


def layer_norm(values):
    center = values - jnp.mean(values, -1, keepdims=True)
    spread = jnp.mean(center * center, -1, keepdims=True)
    return center * lax.rsqrt(spread + 1e-06)


def head_norm(values, gain):
    return values * lax.rsqrt(jnp.mean(values * values, -1, keepdims=True) + 1e-06) * gain


def pick_entry(table, index):
    return lax.dynamic_index_in_dim(table, index, 0, keepdims=False)


def local(
    latents,
    text_hidden,
    w_img_in,
    w_img_qkv,
    w_txt_kv,
    q_gain,
    k_gain,
    w_out,
    w_final,
    mod_img,
    mod_txt,
    mod_final,
    guide,
    step_size,
    img_len,
    txt_len,
    split_flag,
    tstep,
):
    group_index = lax.axis_index("group")
    mp_index = lax.axis_index("mp")
    cfg_index = lax.axis_index("cfg")
    mp_count = lax.axis_size("mp")
    mate_index = jnp.bitwise_xor(group_index, 1)
    step_index = pick_entry(tstep, group_index)
    mod_rows = pick_entry(mod_img, step_index)
    text_rows = pick_entry(mod_txt, step_index)
    final_rows = pick_entry(mod_final, step_index)
    shard_rows = latents.shape[0]
    half_rows = shard_rows // 2
    full_img = shard_rows * mp_count
    full_txt = text_hidden.shape[1] * mp_count
    local_heads = w_img_qkv.shape[1] // (3 * HD)
    x_img = jnp.dot(latents.astype(jnp.bfloat16), w_img_in, preferred_element_type=jnp.float32)
    lat_full = lax.all_gather(latents.astype(jnp.bfloat16), "mp", axis=0, tiled=True)
    x_full = jnp.dot(lat_full, w_img_in, preferred_element_type=jnp.float32)
    img_full = (layer_norm(x_full) * (1.0 + mod_rows[1]) + mod_rows[0]).astype(jnp.bfloat16)
    txt_mod = (
        layer_norm(text_hidden[0].astype(jnp.float32)) * (1.0 + text_rows[1]) + text_rows[0]
    ).astype(jnp.bfloat16)
    txt_full = lax.all_gather(txt_mod, "mp", axis=0, tiled=True)
    qkv = jnp.dot(img_full, w_img_qkv, preferred_element_type=jnp.float32).reshape(
        full_img, local_heads, 3, HD
    )
    query = head_norm(qkv[:, :, 0], q_gain).astype(jnp.bfloat16)
    key_img = head_norm(qkv[:, :, 1], k_gain).astype(jnp.bfloat16)
    value_img = qkv[:, :, 2].astype(jnp.bfloat16)
    text_kv = jnp.dot(txt_full, w_txt_kv, preferred_element_type=jnp.float32).reshape(
        full_txt, local_heads, 2, HD
    )
    key_txt = head_norm(text_kv[:, :, 0], k_gain).astype(jnp.bfloat16)
    value_txt = text_kv[:, :, 1].astype(jnp.bfloat16)
    key_rows = jnp.concatenate([key_txt, key_img], axis=0)
    value_rows = jnp.concatenate([value_txt, value_img], axis=0)
    mate_keys, mate_values = partner((key_rows, value_rows), "group", 0)
    spots_txt = jnp.arange(full_txt, dtype=jnp.int32)
    spots_img = jnp.arange(full_img, dtype=jnp.int32)

    def live_rows(index):
        return jnp.concatenate(
            [spots_txt < pick_entry(txt_len, index), spots_img < pick_entry(img_len, index)]
        )

    flagged = pick_entry(pick_entry(split_flag, cfg_index), group_index) == 1
    live = jnp.concatenate([live_rows(group_index), live_rows(mate_index) & flagged])
    all_keys = jnp.concatenate([key_rows, mate_keys], axis=0)
    all_values = jnp.concatenate([value_rows, mate_values], axis=0)
    scores = jnp.einsum(
        "qhe,khe->hqk", query, all_keys, preferred_element_type=jnp.float32
    ) * HD ** (-0.5)
    scores = jnp.where(live[None, None, :], scores, -1e30)
    weights = jnp.exp(scores - jnp.max(scores, -1, keepdims=True))
    probs = (weights / jnp.sum(weights, -1, keepdims=True)).astype(jnp.bfloat16)
    mixed = jnp.einsum(
        "hqk,khe->qhe", probs, all_values, preferred_element_type=jnp.float32
    ).astype(jnp.bfloat16)
    mixed = mixed.reshape(full_img, local_heads * HD)
    mixed = lax.all_to_all(mixed, "mp", split_axis=0, concat_axis=1, tiled=True)
    attended = jnp.dot(mixed, w_out, preferred_element_type=jnp.float32)
    hidden = x_img + mod_rows[2] * attended
    final = (layer_norm(hidden) * (1.0 + final_rows[1]) + final_rows[0]).astype(jnp.bfloat16)
    own_velocity = jnp.dot(final, w_final, preferred_element_type=jnp.float32)
    scale = pick_entry(guide, group_index)
    other_velocity = partner(own_velocity.astype(jnp.bfloat16), "cfg", 0).astype(own_velocity.dtype)
    is_cond = cfg_index == 0
    cond_part = jnp.where(is_cond, own_velocity, other_velocity)
    uncond_part = jnp.where(is_cond, other_velocity, own_velocity)
    guided_all = uncond_part + scale * (cond_part - uncond_part)
    guided = lax.dynamic_slice_in_dim(guided_all, cfg_index * half_rows, half_rows, 0)
    row_place = (
        mp_index * shard_rows + cfg_index * half_rows + jnp.arange(half_rows, dtype=jnp.int32)
    )
    row_live = row_place < pick_entry(img_len, group_index)
    guided = jnp.where(row_live[:, None], guided, 0.0)
    start_rows = lax.dynamic_slice_in_dim(latents, cfg_index * half_rows, half_rows, 0)
    moved = start_rows - pick_entry(step_size, step_index) * guided
    return (guided[None], moved[None])


def solution(mesh):
    placed = (
        P(("group", "mp"), None),
        P("cfg", ("group", "mp"), None),
        P(),
        P(None, "mp"),
        P(None, "mp"),
        P(),
        P(),
        P(),
        P(),
        P(),
        P(),
        P(),
        P(),
        P(),
        P(),
        P(),
        P(),
        P(),
    )
    return jax.shard_map(
        local,
        mesh=mesh,
        in_specs=placed,
        out_specs=(P("cfg", ("group", "mp"), None), P("cfg", ("group", "mp"), None)),
        check_vma=False,
    )
```

profile of v0, /device:TPU:0, one launch (start us, length us, event | category | flops | bytes accessed | tf_op | source)
XLA Modules:
  0.0 161.9 jit_solution(1764503549173147141)
XLA Ops:
  7.2 1.3 dynamic_slice.48
  9.8 1.3 convert_reduce_fusion
  11.2 1.5 fusion.21
  13.3 1.5 dynamic-slice_add_fusion
  14.8 2.4 %fusion.24 = bf16[128,3072]{1,0:T(8,128)(2,1)} fusion(bf16[1,128,3072]{2,1,0:T(8,128)(2,1)} %param.19, f32[3072]{0:T(1024)S(1)} %bitcast.102, f32[3072]{0:T(1024)S(1)} %bitcast.103, f32[128]{0:T(128)S(1)} %add_rsqrt_fusion.5, f32[128]{0:T(128)S(1)} %broadcast_multiply_fusion.2), kind=kLoop, calls=%fused_computation.35 | loop fusion | flops 2359296 | bytes 1598464 | tf_op jit(solution)/shard_map/convert_element_type | solution.py:69
  17.3 0.6 copy-done.4
  17.9 13.3 %all_gather.7 = bf16[1024,64]{0,1:T(8,128)(2,1)S(1)} all-gather(bf16[256,64]{0,1:T(8,128)(2,1)S(1)} %convert_element_type.51), channel_id=1, replica_groups=mesh['cfg'=2,'group'=16,'mp'=4] {'mp'}, dimensions={0}, use_global_device_ids=true | all-gather | bytes 163840 | tf_op jit(solution)/shard_map/all_gather | solution.py:64
  31.1 6.4 %fusion.52 = (f32[1024]{0:T(1024)S(1)}, f32[1024,3072]{1,0:T(8,128)}) fusion(bf16[1024,64]{0,1:T(8,128)(2,1)S(1)} %all_gather.7, bf16[64,3072]{1,0:T(8,128)(2,1)S(1)} %copy-done), kind=kOutput, calls=%fused_computation.95 | convolution fusion | flops 405797888 | bytes 13111296 | tf_op jit(solution)/shard_map/dot_general | solution.py:65
  37.5 6.0 %multiply_reduce_fusion = f32[1024]{0:T(1024)S(1)} fusion(f32[1024,3072]{1,0:T(8,128)} %get-tuple-element.15, f32[1024]{0:T(1024)S(1)} %broadcast_multiply_fusion), kind=kLoop, calls=%fused_computation.10 | loop fusion | flops 9436160 | bytes 12591104 | tf_op jit(solution)/shard_map/reduce_sum | solution.py:17
  43.6 0.9 fusion.41
  44.5 1.0 constant_dynamic-slice_fusion
  45.5 14.3 %fusion.6 = f32[1024,1152]{0,1:T(8,128)S(1)} fusion(bf16[3072,1152]{1,0:T(8,128)(2,1)} %param.21, f32[1024,3072]{1,0:T(8,128)} %get-tuple-element.15, f32[3072]{0:T(1024)S(1)} %bitcast.108, f32[3072]{0:T(1024)S(1)} %bitcast.107, f32[1024]{0:T(1024)S(1)} %add_rsqrt_fusion.3, f32[1024]{0:T(1024)S(1)} %broadcast_multiply_fusion), kind=kOutput, calls=%fused_computation.11 | convolution fusion | flops 7263485952 | bytes 24412160 | tf_op jit(solution)/shard_map/dot_general | solution.py:71
  59.7 2.1 %copy-done.1 = f32[1024,1152]{0,1:T(8,128)} copy-done((f32[1024,1152]{0,1:T(8,128)}, f32[1024,1152]{0,1:T(8,128)S(1)}, u32[]{:S(2)}) %copy-start.1) | copy-done | bytes 4718616
  62.1 0.5 copy.41
  62.6 1.4 fusion.50
  64.0 0.6 iota_compare_fusion.2
  64.6 0.6 iota_compare_fusion
  65.2 0.7 iota_compare_fusion.1
  65.9 0.5 fusion.25
  66.4 1.1 fusion.27
  67.6 7.3 %fusion.56 = f32[512,768]{1,0:T(8,128)} fusion(bf16[512,3072]{1,0:T(8,128)(2,1)} %all-gather.2.cloned.1.call-done, bf16[3072,768]{1,0:T(8,128)(2,1)} %param.22), kind=kOutput, calls=%fused_computation.99 | convolution fusion | flops 2415919104 | bytes 9437184 | tf_op jit(solution)/shard_map/dot_general | solution.py:77
  74.9 2.1 %reshape.127 = f32[512,3,2,128]{3,2,1,0:T(2,128)S(1)} reshape(f32[512,768]{1,0:T(8,128)} %fusion.56) | data formatting | bytes 3145728 | tf_op jit(solution)/shard_map/reshape | solution.py:77
  77.0 0.5 slice.60
  78.2 1.1 pad_maximum_fusion.2
  79.3 0.7 iota_compare_fusion.3
  80.0 0.6 dynamic_slice.54
  81.3 1.6 multiply_reduce_fusion.2
  82.9 0.6 add_rsqrt_fusion.1
  83.5 1.5 fusion.36
  85.0 0.8 slice.57
  85.8 1.0 copy.42
  86.9 0.6 collective-permute-start
  87.5 19.3 %fusion.53 = (f32[3,1024]{1,0:T(4,128)S(1)}, f32[3,1024,3072]{2,1,0:T(8,128)}) fusion(pred[3072]{0:T(1024)(128)(4,1)S(1)} %pad_add_fusion, bf16[1536,3,128]{2,0,1:T(8,128)(2,1)} %collective-permute-done.1, bf16[1024,3,128]{2,0,1:T(8,128)(2,1)} %copy-done.2, bf16[512,3,128]{2,0,1:T(8,128)(2,1)} %copy-done.3, f32[1024,3,3,128]{0,3,2,1:T(8,128)} %bitcast.99, ...), kind=kOutput, calls=%fused_computation.96 | convolution fusion | flops 2461928448 | bytes 41713152 | tf_op jit(solution)/shard_map/sub | solution.py:101
  106.8 14.9 %fusion.32 = bf16[1024,3,128]{0,2,1:T(8,128)(2,1)S(1)} fusion(f32[3,1024,3072]{2,1,0:T(8,128)} %get-tuple-element.17, f32[3,1024]{1,0:T(4,128)S(1)} %get-tuple-element.16, bf16[1536,3,128]{0,2,1:T(8,128)(2,1)} %collective-permute-done, bf16[1024,3,128]{0,2,1:T(8,128)(2,1)S(1)} %fusion.36, bf16[512,3,128]{0,2,1:T(8,128)(2,1)S(1)} %bitcast.101), kind=kOutput, calls=%fused_computation.47 | convolution fusion | flops 2442264576 | bytes 40906752 | tf_op jit(solution)/shard_map/hqk,khe->qhe/dot_general | solution.py:103
  121.7 0.6 all_to_all.14
  122.3 1.0 copy.33
  123.2 4.3 %all-to-all-start = ((bf16[4,256,384]{1,2,0:T(8,128)(2,1)}), bf16[4,256,384]{1,2,0:T(8,128)(2,1)S(1)}, u32[]{:S(2)}, u32[]{:S(2)}) async-start(bf16[4,256,384]{1,2,0:T(8,128)(2,1)} %copy.33), calls=%async_computation | async-start | bytes 1572864 | tf_op jit(solution)/shard_map/all_to_all | solution.py:107
  127.5 12.5 %all-to-all-done = bf16[4,256,384]{1,2,0:T(8,128)(2,1)S(1)} async-done(((bf16[4,256,384]{1,2,0:T(8,128)(2,1)}), bf16[4,256,384]{1,2,0:T(8,128)(2,1)S(1)}, u32[]{:S(2)}, u32[]{:S(2)}) %all-to-all-start) | async-done | bytes 786464 | tf_op jit(solution)/shard_map/all_to_all | solution.py:107
  140.0 5.2 %convolution_multiply_fusion = f32[256,3072]{1,0:T(8,128)S(1)} fusion(bf16[256,1536]{0,1:T(8,128)(2,1)S(1)} %bitcast.95, bf16[1536,3072]{1,0:T(8,128)(2,1)} %param.25, f32[3072]{0:T(1024)S(1)} %bitcast.104), kind=kOutput, calls=%fused_computation.18 | convolution fusion | flops 2416705536 | bytes 13381632 | tf_op jit(solution)/shard_map/dot_general | solution.py:108
  145.2 0.7 fusion.54
  146.0 0.5 multiply_reduce_fusion.1
  146.6 0.3 copy-done.13
  146.9 0.7 fusion.55
  147.7 3.3 %collective-permute-start.2 = (bf16[256,64]{0,1:T(8,128)(2,1)S(1)}, bf16[256,64]{0,1:T(8,128)(2,1)S(1)}, u32[]{:S(2)}, u32[]{:S(2)}) collective-permute-start(bf16[256,64]{0,1:T(8,128)(2,1)S(1)} %get-tuple-element.20), channel_id=1, source_target_pairs={{0,64},{64,0},{1,65},{65,1},{2,66},{66,2},{3,67},{67,3},{4,68},{68... | collective-permute-start | bytes 98312 | tf_op jit(solution)/shard_map/ppermute | solution.py:12
  151.0 0.7 add_compare_fusion
  151.7 0.7 dynamic_slice.59
  152.3 0.6 dynamic_slice.56
  153.2 1.9 %subtract_bitcast_fusion = (f32[1,128,64]{1,2,0:T(8,128)}, f32[1,128,64]{1,2,0:T(8,128)}) fusion(f32[256,64]{0,1:T(8,128)S(1)} %copy-done.7, s32[]{:T(128)S(6)} %select_n.65, f32[]{:T(128)} %bitcast.25, f32[]{:T(128)} %bitcast.23, f32[256,64]{0,1:T(8,128)S(1)} %get-tuple-element.21, bf16[256,64]{0,1:T(8,128)(2,1)S(1)} %collective-permute-done.2, pred[]{:T(512)S(6)} %eq.9, ...), kind=kLoop, calls=%fused_computation.62 | loop fusion | flops 73728 | bytes 147597 | tf_op jit(solution)/shard_map/broadcast_in_dim | solution.py:126
  (51 shorter events, 1.5 us)
Async XLA Ops:
  7.2 24.0 %copy-start = (bf16[64,3072]{1,0:T(8,128)(2,1)S(1)}, bf16[64,3072]{1,0:T(8,128)(2,1)}, u32[]{:S(2)}) copy-start(bf16[64,3072]{1,0:T(8,128)(2,1)} %param.20) | copy-start | bytes 1179652
  7.2 10.0 %copy-start.6 = (f32[256,64]{0,1:T(8,128)S(1)}, f32[256,64]{0,1:T(8,128)}, u32[]{:S(2)}) copy-start(f32[256,64]{0,1:T(8,128)} %param.18) | copy-start | bytes 196612
  7.2 60.4 %all-gather.2.cloned.1.call-start = ((), (), s32[]{:S(2)}) async-start(), calls=%async_computation.1 | async-start | bytes 3932160 | tf_op jit(solution)/shard_map/all_gather | solution.py:70
  17.2 0.6 copy-start.4
  59.7 2.2 %copy-start.1 = (f32[1024,1152]{0,1:T(8,128)}, f32[1024,1152]{0,1:T(8,128)S(1)}, u32[]{:S(2)}) copy-start(f32[1024,1152]{0,1:T(8,128)S(1)} %fusion.6) | copy-start | bytes 14155780
  61.9 0.7 copy-start.10
  67.6 10.6 %copy-start.2 = (bf16[1024,3,128]{2,0,1:T(8,128)(2,1)}, bf16[1024,3,128]{2,0,1:T(8,128)(2,1)S(1)}, u32[]{:S(2)}) copy-start(bf16[1024,3,128]{2,0,1:T(8,128)(2,1)S(1)} %fusion.27) | copy-start | bytes 2359300
  74.9 3.0 %copy-start.11 = (f32[128]{0:T(128)S(1)}, f32[128]{0:T(128)}, u32[]{:S(2)}) copy-start(f32[128]{0:T(128)} %param.24) | copy-start | bytes 1540
  77.0 3.0 %copy-start.12 = (s32[2,16]{1,0:T(2,128)S(1)}, s32[2,16]{1,0:T(2,128)}, u32[]{:S(2)}) copy-start(s32[2,16]{1,0:T(2,128)} %param.34) | copy-start | bytes 388
  78.2 1.2 copy-start.3
  79.3 8.2 %collective-permute-start.1 = (bf16[1536,3,128]{2,0,1:T(8,128)(2,1)}, bf16[1536,3,128]{2,0,1:T(8,128)(2,1)}, u32[]{:S(2)}, u32[]{:S(2)}) collective-permute-start(bf16[1536,3,128]{2,0,1:T(8,128)(2,1)} %pad_maximum_fusion.2), channel_id=1, source_target_pairs={{0,4},{4,0},{8,12},{12,8},{16,20},{20,16},{24,28},{28,24},{32,36},... | collective-permute-start | bytes 3538952 | tf_op jit(solution)/shard_map/ppermute | solution.py:12
  86.9 19.9 %collective-permute-start = (bf16[1536,3,128]{0,2,1:T(8,128)(2,1)S(1)}, bf16[1536,3,128]{0,2,1:T(8,128)(2,1)}, u32[]{:S(2)}, u32[]{:S(2)}) collective-permute-start(bf16[1536,3,128]{0,2,1:T(8,128)(2,1)S(1)} %pad_maximum_fusion.1), channel_id=1, source_target_pairs={{0,4},{4,0},{8,12},{12,8},{16,20},{20,16},{24,28},{28,24},{32,36},... | collective-permute-start | bytes 3538952 | tf_op jit(solution)/shard_map/ppermute | solution.py:12
  123.2 16.7 %all-to-all-start = ((bf16[4,256,384]{1,2,0:T(8,128)(2,1)}), bf16[4,256,384]{1,2,0:T(8,128)(2,1)S(1)}, u32[]{:S(2)}, u32[]{:S(2)}) async-start(bf16[4,256,384]{1,2,0:T(8,128)(2,1)} %copy.33), calls=%async_computation | async-start | bytes 1572864 | tf_op jit(solution)/shard_map/all_to_all | solution.py:107
  140.0 5.2 %copy-start.5 = (bf16[256,64]{0,1:T(8,128)(2,1)S(1)}, bf16[256,64]{0,1:T(8,128)(2,1)}, u32[]{:S(2)}) copy-start(bf16[256,64]{0,1:T(8,128)(2,1)} %copy-done.4) | copy-start | bytes 98308
  145.9 0.7 copy-start.8
  145.9 0.7 copy-start.9
  145.9 1.0 copy-start.13
  145.9 5.7 %copy-start.14 = (f32[8]{0:T(128)S(1)}, f32[8]{0:T(128)}, u32[]{:S(2)}) copy-start(f32[8]{0:T(128)} %param.31) | copy-start | bytes 100
  145.9 6.4 %copy-start.15 = (f32[16]{0:T(128)S(1)}, f32[16]{0:T(128)}, u32[]{:S(2)}) copy-start(f32[16]{0:T(128)} %param.30) | copy-start | bytes 196
  145.9 7.2 %copy-start.7 = (f32[256,64]{0,1:T(8,128)S(1)}, f32[256,64]{0,1:T(8,128)}, u32[]{:S(2)}) copy-start(f32[256,64]{0,1:T(8,128)} %param.18) | copy-start | bytes 196612
  147.7 5.5 %collective-permute-start.2 = (bf16[256,64]{0,1:T(8,128)(2,1)S(1)}, bf16[256,64]{0,1:T(8,128)(2,1)S(1)}, u32[]{:S(2)}, u32[]{:S(2)}) collective-permute-start(bf16[256,64]{0,1:T(8,128)(2,1)S(1)} %get-tuple-element.20), channel_id=1, source_target_pairs={{0,64},{64,0},{1,65},{65,1},{2,66},{66,2},{3,67},{67,3},{4,68},{68... | collective-permute-start | bytes 98312 | tf_op jit(solution)/shard_map/ppermute | solution.py:12
Sparse Core Ops, SparseCore 0:
  17.3 42.2 all-gather.1
where the time goes:
time: 163 us; the launch traced here: 162 us
  matrix products  68.8 us (42%)
  other arithmetic  24.9 us (15%)
  between operations  17.1 us (10%)
  local copies, waits for them, and re-layouts  17 us (10%)
  blocking collectives  13.3 us (8%)
  waiting for transfers between devices  12.8 us (8%)
  starting transfers between devices  8.17 us (5%)
    sub x1, matrix products, local(): weights = jnp.exp(scores - jnp.max(scores, -1, keepdims=True))  19.3 us
    dot_general x1, matrix products, local(): jnp.einsum('hqk,khe->qhe', probs, all_values, preferred_element_type=jnp....  14.9 us
    dot_general x1, matrix products, local(): jnp.dot(img_full, w_img_qkv, preferred_element_type=jnp.float32)  14.3 us
    all_gather x1, blocking collectives, local(): lax.all_gather(latents.astype(jnp.bfloat16), 'mp', axis=0, tiled=True)  13.3 us
    all_to_all x1, waiting for transfers between devices, local(): mixed = lax.all_to_all(mixed, 'mp', split_axis=0, concat_axis=1, tiled=True)  12.5 us
    reduce_sum x3, other arithmetic, layer_norm(): spread = jnp.mean(center * center, -1, keepdims=True)  7.98 us
    dot_general x1, matrix products, local(): jnp.dot(txt_full, w_txt_kv, preferred_element_type=jnp.float32)  7.3 us
    dot_general x1, matrix products, local(): x_full = jnp.dot(lat_full, w_img_in, preferred_element_type=jnp.float32)  6.4 us
  transfers between devices with their start and end apart: 5, of which 2 were waited for; matrix products, arithmetic and copies ran while one was open for 38% of the time, Pallas kernels for 0%

commit v1 on v0

--- a/solution.py
+++ b/solution.py
@@ -61,7 +61,10 @@
     full_txt = text_hidden.shape[1] * mp_count
     local_heads = w_img_qkv.shape[1] // (3 * HD)
     x_img = jnp.dot(latents.astype(jnp.bfloat16), w_img_in, preferred_element_type=jnp.float32)
-    lat_full = lax.all_gather(latents.astype(jnp.bfloat16), "mp", axis=0, tiled=True)
+    lat_full = jnp.concatenate(
+        lax.all_to_all(jnp.stack([latents.astype(jnp.bfloat16)] * lax.axis_size("mp")), "mp", 0, 0),
+        axis=0,
+    )
     x_full = jnp.dot(lat_full, w_img_in, preferred_element_type=jnp.float32)
     img_full = (layer_norm(x_full) * (1.0 + mod_rows[1]) + mod_rows[0]).astype(jnp.bfloat16)
     txt_mod = (

time: 163 us -> 160 us (0.982)
  blocking collectives: 13.3 us -> 0 us
  waiting for transfers between devices: 12.8 us -> 23.6 us
  matrix products: 68.8 us -> 63.7 us
  starting transfers between devices: 8.17 us -> 12.6 us
  local copies, waits for them, and re-layouts: 17 us -> 20.4 us
  other arithmetic: 24.9 us -> 22 us
    all_gather x1 -> x0, blocking collectives: 13.3 us -> none  [local(): lax.all_gather(latents.astype(jnp.bfloat16), 'mp', axis=0, tiled=True)]
    all_gather x1, waiting for transfers between devices: 0.02 us -> 10.3 us  [local(): txt_full = lax.all_gather(txt_mod, 'mp', axis=0, tiled=True)]
    all_to_all x0 -> x1, starting transfers between devices: none -> 5.39 us  [local(): lax.all_to_all(jnp.stack([latents.astype(jnp.bfloat16)] * lax.axis_size('...]
    reduce_sum x3, other arithmetic: 7.98 us -> 3.32 us  [layer_norm(): spread = jnp.mean(center * center, -1, keepdims=True)]
    dot_general x1, matrix products: 6.4 us -> 1.91 us  [local(): x_full = jnp.dot(lat_full, w_img_in, preferred_element_type=jnp.float32)]
    unnamed x34 -> x42, local copies, waits for them, and re-layouts: 4.78 us -> 8.37 us
  transfers between devices with their start and end apart: 5 -> 6, of which waited for: 2 -> 3; matrix products, arithmetic and copies ran while one was open for 38% -> 38% of each run, Pallas kernels for 0% -> 0%
where the time goes in v1:
time: 160 us; the launch traced here: 159 us
  matrix products  63.7 us (40%)
  waiting for transfers between devices  23.6 us (15%)
  other arithmetic  22 us (14%)
  local copies, waits for them, and re-layouts  20.4 us (13%)
  between operations  17 us (11%)
  starting transfers between devices  12.6 us (8%)
    sub x1, matrix products, local(): weights = jnp.exp(scores - jnp.max(scores, -1, keepdims=True))  19.3 us
    dot_general x1, matrix products, local(): jnp.einsum('hqk,khe->qhe', probs, all_values, preferred_element_type=jnp....  14.8 us
    dot_general x1, matrix products, local(): jnp.dot(img_full, w_img_qkv, preferred_element_type=jnp.float32)  14 us
    all_to_all x1, waiting for transfers between devices, local(): mixed = lax.all_to_all(mixed, 'mp', split_axis=0, concat_axis=1, tiled=True)  12.7 us
    all_gather x1, waiting for transfers between devices, local(): txt_full = lax.all_gather(txt_mod, 'mp', axis=0, tiled=True)  10.3 us
    unnamed x42, local copies, waits for them, and re-layouts  8.37 us
    dot_general x1, matrix products, local(): jnp.dot(txt_full, w_txt_kv, preferred_element_type=jnp.float32)  7.05 us
    all_to_all x1, starting transfers between devices, local(): lax.all_to_all(jnp.stack([latents.astype(jnp.bfloat16)] * lax.axis_size('...  5.39 us
  transfers between devices with their start and end apart: 6, of which 3 were waited for; matrix products, arithmetic and copies ran while one was open for 38% of the time, Pallas kernels for 0%

profile of v1, /device:TPU:0, one launch (start us, length us, event | category | flops | bytes accessed | tf_op | source)
XLA Modules:
  0.0 159.4 jit_solution(1150286668375766908)
XLA Ops:
  7.2 0.9 convert_element_type.51
  8.1 0.6 copy-done.5
  8.7 0.7 stack.2
  9.4 5.4 %all-to-all-start = ((bf16[4,256,64]{1,2,0:T(8,128)(2,1)}), bf16[4,256,64]{1,2,0:T(8,128)(2,1)S(1)}, u32[]{:S(2)}, u32[]{:S(2)}) async-start(bf16[4,256,64]{1,2,0:T(8,128)(2,1)} %stack.2), calls=%async_computation | async-start | bytes 262144 | tf_op jit(solution)/shard_map/all_to_all | solution.py:65
  14.8 1.2 dynamic_slice.48
  17.3 1.3 convert_reduce_fusion
  18.6 1.5 fusion.21
  20.8 0.8 dynamic-slice_add_fusion.1
  21.6 2.4 %fusion.24 = bf16[128,3072]{1,0:T(8,128)(2,1)} fusion(bf16[1,128,3072]{2,1,0:T(8,128)(2,1)} %param.19, f32[3072]{0:T(1024)S(1)} %bitcast.108, f32[3072]{0:T(1024)S(1)} %bitcast.107, f32[128]{0:T(128)S(1)} %add_rsqrt_fusion.5, f32[128]{0:T(128)S(1)} %broadcast_multiply_fusion.2), kind=kLoop, calls=%fused_computation.35 | loop fusion | flops 2359296 | bytes 1598464 | tf_op jit(solution)/shard_map/convert_element_type | solution.py:72
  24.1 1.6 dynamic-slice_add_fusion
  25.7 1.0 constant_dynamic-slice_fusion
  26.6 0.7 fusion.50
  27.3 1.2 iota_compare_fusion
  28.5 1.2 iota_compare_fusion.1
  29.7 1.1 iota_compare_fusion.2
  30.9 1.9 %fusion.52 = (f32[1024]{0:T(1024)S(1)}, f32[1024,3072]{1,0:T(8,128)S(1)}) fusion(bf16[1024,64]{0,1:T(8,128)(2,1)S(1)} %bitcast.104, bf16[64,3072]{1,0:T(8,128)(2,1)S(1)} %copy-done), kind=kOutput, calls=%fused_computation.95 | convolution fusion | flops 405797888 | bytes 13111296 | tf_op jit(solution)/shard_map/dot_general | solution.py:68
  32.8 1.4 multiply_reduce_fusion
  34.2 3.6 %copy-done.1 = f32[1024,3072]{1,0:T(8,128)} copy-done((f32[1024,3072]{1,0:T(8,128)}, f32[1024,3072]{1,0:T(8,128)S(1)}, u32[]{:S(2)}) %copy-start.1) | copy-done | bytes 12582936
  37.7 14.0 %fusion.6 = f32[1024,1152]{0,1:T(8,128)S(1)} fusion(bf16[3072,1152]{1,0:T(8,128)(2,1)} %param.21, f32[1024,3072]{1,0:T(8,128)} %copy-done.1, f32[3072]{0:T(1024)S(1)} %bitcast.112, f32[3072]{0:T(1024)S(1)} %bitcast.111, f32[1024]{0:T(1024)S(1)} %add_rsqrt_fusion.3, f32[1024]{0:T(1024)S(1)} %broadcast_multiply_fusion), kind=kOutput, calls=%fused_computation.11 | convolution fusion | flops 7263485952 | bytes 24412160 | tf_op jit(solution)/shard_map/dot_general | solution.py:74
  51.7 2.1 %copy-done.2 = f32[1024,1152]{0,1:T(8,128)} copy-done((f32[1024,1152]{0,1:T(8,128)}, f32[1024,1152]{0,1:T(8,128)S(1)}, u32[]{:S(2)}) %copy-start.2) | copy-done | bytes 4718616
  55.6 10.3 %all-gather.2.cloned.1.call-done = bf16[512,3072]{1,0:T(8,128)(2,1)} async-done(((bf16[128,3072]{1,0:T(8,128)(2,1)}), bf16[512,3072]{1,0:T(8,128)(2,1)}) %all-gather.2.cloned.1.call-update) | async-done | bytes 3145744 | tf_op jit(solution)/shard_map/all_gather | solution.py:73
  65.9 7.0 %fusion.56 = f32[512,768]{1,0:T(8,128)} fusion(bf16[512,3072]{1,0:T(8,128)(2,1)} %all-gather.2.cloned.1.call-done, bf16[3072,768]{1,0:T(8,128)(2,1)} %param.22), kind=kOutput, calls=%fused_computation.99 | convolution fusion | flops 2415919104 | bytes 9437184 | tf_op jit(solution)/shard_map/dot_general | solution.py:80
  72.9 2.1 %reshape.132 = f32[512,3,2,128]{3,2,1,0:T(2,128)S(1)} reshape(f32[512,768]{1,0:T(8,128)} %fusion.56) | data formatting | bytes 3145728 | tf_op jit(solution)/shard_map/reshape | solution.py:80
  75.1 0.5 slice.60
  76.2 1.2 pad_maximum_fusion.2
  77.4 0.6 iota_compare_fusion.3
  78.0 0.6 dynamic_slice.54
  79.2 1.6 multiply_reduce_fusion.2
  80.8 0.6 add_rsqrt_fusion.1
  81.4 1.5 fusion.36
  82.9 0.8 slice.57
  83.8 1.0 copy.61
  84.9 0.6 collective-permute-start
  85.4 19.3 %fusion.53 = (f32[3,1024]{1,0:T(4,128)S(1)}, f32[3,1024,3072]{2,1,0:T(8,128)}) fusion(pred[3072]{0:T(1024)(128)(4,1)S(1)} %pad_add_fusion, bf16[1536,3,128]{2,0,1:T(8,128)(2,1)} %collective-permute-done.1, bf16[1024,3,128]{2,0,1:T(8,128)(2,1)} %copy-done.3, bf16[512,3,128]{2,0,1:T(8,128)(2,1)} %copy-done.4, f32[1024,3,3,128]{0,3,2,1:T(8,128)} %bitcast.101, ...), kind=kOutput, calls=%fused_computation.96 | convolution fusion | flops 2461928448 | bytes 41713152 | tf_op jit(solution)/shard_map/sub | solution.py:104
  104.8 14.8 %fusion.32 = bf16[1024,3,128]{0,2,1:T(8,128)(2,1)S(1)} fusion(f32[3,1024,3072]{2,1,0:T(8,128)} %get-tuple-element.17, f32[3,1024]{1,0:T(4,128)S(1)} %get-tuple-element.16, bf16[1536,3,128]{0,2,1:T(8,128)(2,1)} %collective-permute-done, bf16[1024,3,128]{0,2,1:T(8,128)(2,1)S(1)} %fusion.36, bf16[512,3,128]{0,2,1:T(8,128)(2,1)S(1)} %bitcast.103), kind=kOutput, calls=%fused_computation.47 | convolution fusion | flops 2442264576 | bytes 40906752 | tf_op jit(solution)/shard_map/hqk,khe->qhe/dot_general | solution.py:106
  119.6 0.6 all_to_all.18
  120.2 1.0 copy.52
  121.2 3.5 %all-to-all-start.1 = ((bf16[4,256,384]{1,2,0:T(8,128)(2,1)}), bf16[4,256,384]{1,2,0:T(8,128)(2,1)S(1)}, u32[]{:S(2)}, u32[]{:S(2)}) async-start(bf16[4,256,384]{1,2,0:T(8,128)(2,1)} %copy.52), calls=%async_computation.1 | async-start | bytes 1572864 | tf_op jit(solution)/shard_map/all_to_all | solution.py:110
  124.7 12.7 %all-to-all-done.1 = bf16[4,256,384]{1,2,0:T(8,128)(2,1)S(1)} async-done(((bf16[4,256,384]{1,2,0:T(8,128)(2,1)}), bf16[4,256,384]{1,2,0:T(8,128)(2,1)S(1)}, u32[]{:S(2)}, u32[]{:S(2)}) %all-to-all-start.1) | async-done | bytes 786464 | tf_op jit(solution)/shard_map/all_to_all | solution.py:110
  137.4 5.2 %convolution_multiply_fusion = f32[256,3072]{1,0:T(8,128)S(1)} fusion(bf16[256,1536]{0,1:T(8,128)(2,1)S(1)} %bitcast.97, bf16[1536,3072]{1,0:T(8,128)(2,1)} %param.25, f32[3072]{0:T(1024)S(1)} %bitcast.106), kind=kOutput, calls=%fused_computation.18 | convolution fusion | flops 2416705536 | bytes 13381632 | tf_op jit(solution)/shard_map/dot_general | solution.py:111
  142.7 0.7 fusion.54
  144.4 0.7 fusion.55
  145.1 3.1 %collective-permute-start.2 = (bf16[256,64]{0,1:T(8,128)(2,1)S(1)}, bf16[256,64]{0,1:T(8,128)(2,1)S(1)}, u32[]{:S(2)}, u32[]{:S(2)}) collective-permute-start(bf16[256,64]{0,1:T(8,128)(2,1)S(1)} %get-tuple-element.20), channel_id=1, source_target_pairs={{0,64},{64,0},{1,65},{65,1},{2,66},{66,2},{3,67},{67,3},{4,68},{68... | collective-permute-start | bytes 98312 | tf_op jit(solution)/shard_map/ppermute | solution.py:12
  148.2 0.6 add_compare_fusion
  148.9 0.7 dynamic_slice.59
  149.5 0.6 dynamic_slice.56
  150.1 0.5 collective-permute-done.2
  150.6 1.9 %subtract_bitcast_fusion = (f32[1,128,64]{1,2,0:T(8,128)}, f32[1,128,64]{1,2,0:T(8,128)}) fusion(f32[256,64]{0,1:T(8,128)S(1)} %copy-done.7, s32[]{:T(128)S(6)} %select_n.65, f32[]{:T(128)} %bitcast.25, f32[]{:T(128)} %bitcast.23, f32[256,64]{0,1:T(8,128)S(1)} %get-tuple-element.21, bf16[256,64]{0,1:T(8,128)(2,1)S(1)} %collective-permute-done.2, pred[]{:T(512)S(6)} %eq.9, ...), kind=kLoop, calls=%fused_computation.62 | loop fusion | flops 73728 | bytes 147597 | tf_op jit(solution)/shard_map/broadcast_in_dim | solution.py:129
  (62 shorter events, 3.4 us)
Async XLA Ops:
  7.2 23.7 %copy-start = (bf16[64,3072]{1,0:T(8,128)(2,1)S(1)}, bf16[64,3072]{1,0:T(8,128)(2,1)}, u32[]{:S(2)}) copy-start(bf16[64,3072]{1,0:T(8,128)(2,1)} %param.20) | copy-start | bytes 1179652
  7.2 19.4 %copy-start.11 = (s32[16]{0:T(128)S(1)}, s32[16]{0:T(128)}, u32[]{:S(2)}) copy-start(s32[16]{0:T(128)} %param.32) | copy-start | bytes 196
  7.2 19.4 %copy-start.10 = (s32[16]{0:T(128)S(1)}, s32[16]{0:T(128)}, u32[]{:S(2)}) copy-start(s32[16]{0:T(128)} %param.33) | copy-start | bytes 196
  8.1 0.6 copy-start.5
  9.4 21.5 %all-to-all-start = ((bf16[4,256,64]{1,2,0:T(8,128)(2,1)}), bf16[4,256,64]{1,2,0:T(8,128)(2,1)S(1)}, u32[]{:S(2)}, u32[]{:S(2)}) async-start(bf16[4,256,64]{1,2,0:T(8,128)(2,1)} %stack.2), calls=%async_computation | async-start | bytes 262144 | tf_op jit(solution)/shard_map/all_to_all | solution.py:65
  14.8 51.1 %all-gather.2.cloned.1.call-start = ((), (), s32[]{:S(2)}) async-start(), calls=%async_computation.2 | async-start | bytes 3932160 | tf_op jit(solution)/shard_map/all_gather | solution.py:73
  32.8 5.0 %copy-start.1 = (f32[1024,3072]{1,0:T(8,128)}, f32[1024,3072]{1,0:T(8,128)S(1)}, u32[]{:S(2)}) copy-start(f32[1024,3072]{1,0:T(8,128)S(1)} %get-tuple-element.15) | copy-start | bytes 37748740
  51.7 2.2 %copy-start.2 = (f32[1024,1152]{0,1:T(8,128)}, f32[1024,1152]{0,1:T(8,128)S(1)}, u32[]{:S(2)}) copy-start(f32[1024,1152]{0,1:T(8,128)S(1)} %fusion.6) | copy-start | bytes 14155780
  54.1 1.0 copy-start.12
  55.5 20.6 %copy-start.3 = (bf16[1024,3,128]{2,0,1:T(8,128)(2,1)}, bf16[1024,3,128]{2,0,1:T(8,128)(2,1)S(1)}, u32[]{:S(2)}) copy-start(bf16[1024,3,128]{2,0,1:T(8,128)(2,1)S(1)} %fusion.27) | copy-start | bytes 2359300
  75.0 3.0 %copy-start.16 = (s32[2,16]{1,0:T(2,128)S(1)}, s32[2,16]{1,0:T(2,128)}, u32[]{:S(2)}) copy-start(s32[2,16]{1,0:T(2,128)} %param.34) | copy-start | bytes 388
  75.0 4.1 %copy-start.14 = (pred[1024]{0:T(1024)(128)(4,1)S(1)}, pred[1024]{0:T(1024)(128)(4,1)}, u32[]{:S(2)}) copy-start(pred[1024]{0:T(1024)(128)(4,1)} %iota_compare_fusion) | copy-start | bytes 3076
  75.0 4.1 %copy-start.15 = (pred[512]{0:T(512)(128)(4,1)S(1)}, pred[512]{0:T(512)(128)(4,1)}, u32[]{:S(2)}) copy-start(pred[512]{0:T(512)(128)(4,1)} %iota_compare_fusion.2) | copy-start | bytes 1540
  75.0 4.2 %copy-start.13 = (pred[1024]{0:T(1024)(128)(4,1)S(1)}, pred[1024]{0:T(1024)(128)(4,1)}, u32[]{:S(2)}) copy-start(pred[1024]{0:T(1024)(128)(4,1)} %iota_compare_fusion.1) | copy-start | bytes 3076
  76.2 1.2 copy-start.4
  77.4 8.1 %collective-permute-start.1 = (bf16[1536,3,128]{2,0,1:T(8,128)(2,1)}, bf16[1536,3,128]{2,0,1:T(8,128)(2,1)}, u32[]{:S(2)}, u32[]{:S(2)}) collective-permute-start(bf16[1536,3,128]{2,0,1:T(8,128)(2,1)} %pad_maximum_fusion.2), channel_id=1, source_target_pairs={{0,4},{4,0},{8,12},{12,8},{16,20},{20,16},{24,28},{28,24},{32,36},... | collective-permute-start | bytes 3538952 | tf_op jit(solution)/shard_map/ppermute | solution.py:12
  84.9 19.9 %collective-permute-start = (bf16[1536,3,128]{0,2,1:T(8,128)(2,1)S(1)}, bf16[1536,3,128]{0,2,1:T(8,128)(2,1)}, u32[]{:S(2)}, u32[]{:S(2)}) collective-permute-start(bf16[1536,3,128]{0,2,1:T(8,128)(2,1)S(1)} %pad_maximum_fusion.1), channel_id=1, source_target_pairs={{0,4},{4,0},{8,12},{12,8},{16,20},{20,16},{24,28},{28,24},{32,36},... | collective-permute-start | bytes 3538952 | tf_op jit(solution)/shard_map/ppermute | solution.py:12
  121.2 16.2 %all-to-all-start.1 = ((bf16[4,256,384]{1,2,0:T(8,128)(2,1)}), bf16[4,256,384]{1,2,0:T(8,128)(2,1)S(1)}, u32[]{:S(2)}, u32[]{:S(2)}) async-start(bf16[4,256,384]{1,2,0:T(8,128)(2,1)} %copy.52), calls=%async_computation.1 | async-start | bytes 1572864 | tf_op jit(solution)/shard_map/all_to_all | solution.py:110
  137.4 5.2 %copy-start.6 = (bf16[256,64]{0,1:T(8,128)(2,1)S(1)}, bf16[256,64]{0,1:T(8,128)(2,1)}, u32[]{:S(2)}) copy-start(bf16[256,64]{0,1:T(8,128)(2,1)} %copy-done.5) | copy-start | bytes 98308
  143.3 0.7 copy-start.8
  143.3 0.7 copy-start.9
  143.3 1.0 copy-start.17
  143.4 5.5 %copy-start.18 = (f32[8]{0:T(128)S(1)}, f32[8]{0:T(128)}, u32[]{:S(2)}) copy-start(f32[8]{0:T(128)} %param.31) | copy-start | bytes 100
  143.4 6.2 %copy-start.19 = (f32[16]{0:T(128)S(1)}, f32[16]{0:T(128)}, u32[]{:S(2)}) copy-start(f32[16]{0:T(128)} %param.30) | copy-start | bytes 196
  143.4 7.2 %copy-start.7 = (f32[256,64]{0,1:T(8,128)S(1)}, f32[256,64]{0,1:T(8,128)}, u32[]{:S(2)}) copy-start(f32[256,64]{0,1:T(8,128)} %param.18) | copy-start | bytes 196612
  145.1 5.5 %collective-permute-start.2 = (bf16[256,64]{0,1:T(8,128)(2,1)S(1)}, bf16[256,64]{0,1:T(8,128)(2,1)S(1)}, u32[]{:S(2)}, u32[]{:S(2)}) collective-permute-start(bf16[256,64]{0,1:T(8,128)(2,1)S(1)} %get-tuple-element.20), channel_id=1, source_target_pairs={{0,64},{64,0},{1,65},{65,1},{2,66},{66,2},{3,67},{67,3},{4,68},{68... | collective-permute-start | bytes 98312 | tf_op jit(solution)/shard_map/ppermute | solution.py:12
Sparse Core Ops, SparseCore 0:
  24.2 41.6 all-gather.1
